TPU v7x, 128 devices: a whole 4x4x4 slice. The times are simulated.
128 devices in a mesh: lm: 8 (over z, x_hi), sl: 16 (over y, x_lo, core).
Axes of the slice: x: 4 (x_hi: 2, x_lo: 2; x = x_hi * 2 + x_lo), y: 4, z: 4, core: 2. Of those that a mesh axis runs over, the one named last changes fastest.
Arguments:
- slab: bfloat16 [16384, 1024], P('sl'), may hold values from -6 to 6
- landmarks: bfloat16 [32768, 1024], P(('lm', 'sl')), may hold values from -6 to 6
- codes: bfloat16 [32768, 96], P(('lm', 'sl')), may hold values from -4 to 4
- exponents: int32 [256], P(('lm', 'sl')), may hold values from -3 to 3
- eigvec: bfloat16 [96, 64], replicated, may hold values from -0.625 to 0.625
- ritz: float32 [64], replicated, may hold values from 0.5 to 4
Outputs:
- extended: float32 [16384, 64], P('sl')
All inputs are finite; a program needn't handle non-finite values.
Results may differ from a plain program's by a relative error of at most 0.004.
Values may be sent and summed in bfloat16 or wider, within the bound.
A program may use at most 128 MiB of HBM per device.

v0:
```python
import math
import jax
import jax.numpy as jnp
from jax import lax
from jax.sharding import PartitionSpec as P

BLOCK = 128


def affinity_sum(rows, land_piece, vec_piece, coeff):
    scores = jnp.dot(rows, land_piece.T, preferred_element_type=jnp.float32) * coeff
    affinity = jnp.exp(scores).astype(jnp.bfloat16)
    return jnp.dot(affinity, vec_piece, preferred_element_type=jnp.float32)


def local(slab, landmarks, codes, exponents, eigvec, ritz):
    total_land = codes.shape[0] * lax.axis_size("lm") * lax.axis_size("sl")
    coeff = 1.0 / math.sqrt(slab.shape[1])
    factor = 1.0 / (ritz * math.sqrt(total_land))
    scale = jnp.exp2(exponents.astype(jnp.float32))
    rows_scale = jnp.repeat(scale, BLOCK)
    basis = (codes.astype(jnp.float32) * rows_scale[:, None]).astype(jnp.bfloat16)
    vectors = jnp.dot(basis, eigvec, preferred_element_type=jnp.float32).astype(jnp.bfloat16)
    terms = affinity_sum(lax.all_gather(slab, "sl", axis=0, tiled=True), landmarks, vectors, coeff)
    partial_sum = lax.psum_scatter(terms, "sl", scatter_dimension=0, tiled=True)
    summed = lax.psum(partial_sum, "lm")
    return summed * factor[None, :]


def solution(mesh):
    return jax.shard_map(
        local,
        mesh=mesh,
        in_specs=(
            P("sl", None),
            P(("lm", "sl"), None),
            P(("lm", "sl"), None),
            P(("lm", "sl")),
            P(),
            P(),
        ),
        out_specs=P("sl", None),
        check_vma=False,
    )
```

profile of v0, /device:TPU:0, one launch (start us, length us, event | category | flops | bytes accessed | tf_op | source)
XLA Modules:
  0.0 365.8 jit_solution(13882836581902991858)
XLA Ops:
  6.5 0.0 copy-start
  6.5 0.0 all-gather.2.cloned.1.call-start
  6.5 0.7 all-gather.2.cloned.1.call-update
  7.3 0.0 reduce-scatter.2.cloned.1.call-start
  7.3 0.7 multiply_exponential_fusion
  8.0 0.1 broadcast_bitcast_fusion
  8.0 1.0 convolution_convert_fusion
  9.0 0.0 copy-start.1
  9.0 173.1 %all-gather.2.cloned.1.call-done = bf16[16384,1024]{1,0:T(8,128)(2,1)} async-done(((bf16[1024,1024]{1,0:T(8,128)(2,1)}), bf16[16384,1024]{1,0:T(8,128)(2,1)}) %all-gather.2.cloned.1.call-update) | async-done | bytes 33554448 | tf_op jit(solution)/shard_map/all_gather | solution.py:24
  182.1 0.0 copy-done
  182.1 18.8 %fusion.2 = f32[16384,64]{0,1:T(8,128)} fusion(bf16[256,64]{1,0:T(8,128)(2,1)S(1)} %convolution_convert_fusion, bf16[16384,1024]{1,0:T(8,128)(2,1)} %all-gather.2.cloned.1.call-done, bf16[256,1024]{1,0:T(8,128)(2,1)S(1)} %copy-done), kind=kOutput, calls=%fused_computation.3 | convolution fusion | flops 9135194112 | bytes 38305792 | tf_op jit(solution)/shard_map/dot_general | solution.py:13
  201.0 0.0 reduce-scatter.2.cloned.1.call-update
  201.0 0.0 all-reduce.2.cloned.1.call-start
  201.1 70.5 %reduce-scatter.2.cloned.1.call-done = f32[1024,64]{0,1:T(8,128)} async-done(((f32[16384,64]{0,1:T(8,128)}), f32[1024,64]{0,1:T(8,128)}) %reduce-scatter.2.cloned.1.call-update) | async-done | bytes 262160 | tf_op jit(solution)/shard_map/reduce_scatter | solution.py:25
  271.5 0.0 all-reduce.2.cloned.1.call-update
  271.6 0.0 copy-done.1
  271.6 85.9 %all-reduce.2.cloned.1.call-done = f32[1024,64]{0,1:T(8,128)} async-done(((f32[1024,64]{0,1:T(8,128)}), f32[1024,64]{0,1:T(8,128)}) %all-reduce.2.cloned.1.call-update) | async-done | bytes 262160 | tf_op jit(solution)/shard_map/psum | solution.py:26
  357.5 1.7 broadcast_multiply_fusion
  (1 shorter events, 0.0 us)
Async XLA Ops:
  6.5 175.6 %copy-start = (bf16[256,1024]{1,0:T(8,128)(2,1)S(1)}, bf16[256,1024]{1,0:T(8,128)(2,1)}, u32[]{:S(2)}) copy-start(bf16[256,1024]{1,0:T(8,128)(2,1)} %param.7) | copy-start | bytes 1572868
  6.5 175.6 %all-gather.2.cloned.1.call-start = ((), (), s32[]{:S(2)}) async-start(), calls=%async_computation.1 | async-start | bytes 35651584 | tf_op jit(solution)/shard_map/all_gather | solution.py:24
  7.3 264.3 %reduce-scatter.2.cloned.1.call-start = ((), (), s32[]{:S(2)}) async-start(), calls=%async_computation.2 | async-start | bytes 4456448 | tf_op jit(solution)/shard_map/reduce_scatter | solution.py:25
  9.0 262.5 %copy-start.1 = (f32[64]{0:T(128)S(1)}, f32[64]{0:T(128)}, u32[]{:S(2)}) copy-start(f32[64]{0:T(128)} %param.11) | copy-start | bytes 772
  201.0 156.5 %all-reduce.2.cloned.1.call-start = ((), (), s32[]{:S(2)}) async-start(), calls=%async_computation.3 | async-start | bytes 524288 | tf_op jit(solution)/shard_map/psum | solution.py:26
Sparse Core Ops, SparseCore 0:
  9.1 173.0 all-gather.1
  201.1 70.3 reduce-scatter.1
  274.0 83.4 all-reduce.1
where the time goes:
time: 366 us
  waiting for transfers between devices  330 us (90%)
  matrix products  19.8 us (5%)
  between operations  13.1 us (4%)
    all_gather x1, waiting for transfers between devices, local(): lax.all_gather(slab, 'sl', axis=0, tiled=True)  173 us
    psum x1, waiting for transfers between devices, local(): summed = lax.psum(partial_sum, 'lm')  85.9 us
    reduce_scatter x1, waiting for transfers between devices, local(): partial_sum = lax.psum_scatter(terms, 'sl', scatter_dimension=0, tiled=True)  70.5 us
    dot_general x1, matrix products, affinity_sum(): return jnp.dot(affinity, vec_piece, preferred_element_type=jnp.float32)  18.8 us
  transfers between devices with their start and end apart: 3, of which 3 were waited for; matrix products, arithmetic and copies ran while one was open for 0% of the time, Pallas kernels for 0%

commit v1 on v0

--- a/solution.py
+++ b/solution.py
@@ -5,6 +5,12 @@
 from jax.sharding import PartitionSpec as P
 
 BLOCK = 128
+
+
+def add_all(x, name):
+    pieces = lax.all_gather(x, name, axis=0, tiled=False)
+    result = pieces.sum(axis=0)
+    return result
 
 
 def affinity_sum(rows, land_piece, vec_piece, coeff):
@@ -23,7 +29,7 @@
     vectors = jnp.dot(basis, eigvec, preferred_element_type=jnp.float32).astype(jnp.bfloat16)
     terms = affinity_sum(lax.all_gather(slab, "sl", axis=0, tiled=True), landmarks, vectors, coeff)
     partial_sum = lax.psum_scatter(terms, "sl", scatter_dimension=0, tiled=True)
-    summed = lax.psum(partial_sum, "lm")
+    summed = add_all(partial_sum, "lm")
     return summed * factor[None, :]
 
 

time: 366 us -> 338 us (0.923)
  waiting for transfers between devices: 330 us -> 300 us
    psum x1 -> x0, waiting for transfers between devices: 85.9 us -> none  [local(): summed = lax.psum(partial_sum, 'lm')]
    all_gather x0 -> x1, waiting for transfers between devices: none -> 55.3 us  [add_all(): pieces = lax.all_gather(x, name, axis=0, tiled=False)]
  transfers between devices with their start and end apart: 3 -> 3, of which waited for: 3 -> 3; matrix products, arithmetic and copies ran while one was open for 0% -> 1% of each run, Pallas kernels for 0% -> 0%
where the time goes in v1:
time: 338 us; the launch traced here: 337 us
  waiting for transfers between devices  300 us (89%)
  matrix products  19.8 us (6%)
  between operations  13.1 us (4%)
    all_gather x1, waiting for transfers between devices, local(): lax.all_gather(slab, 'sl', axis=0, tiled=True)  173 us
    reduce_scatter x1, waiting for transfers between devices, local(): partial_sum = lax.psum_scatter(terms, 'sl', scatter_dimension=0, tiled=True)  70.5 us
    all_gather x1, waiting for transfers between devices, add_all(): pieces = lax.all_gather(x, name, axis=0, tiled=False)  55.3 us
    dot_general x1, matrix products, affinity_sum(): return jnp.dot(affinity, vec_piece, preferred_element_type=jnp.float32)  18.8 us
  transfers between devices with their start and end apart: 3, of which 3 were waited for; matrix products, arithmetic and copies ran while one was open for 1% of the time, Pallas kernels for 0%

profile of v1, /device:TPU:0, one launch (start us, length us, event | category | flops | bytes accessed | tf_op | source)
XLA Modules:
  0.0 337.5 jit_solution(5185767268095954319)
XLA Ops:
  6.5 0.0 copy-start
  6.5 0.0 all-gather.4.cloned.1.call-start
  6.5 0.7 all-gather.4.cloned.1.call-update
  7.3 0.0 reduce-scatter.2.cloned.1.call-start
  7.3 0.7 multiply_exponential_fusion
  8.0 0.1 broadcast_bitcast_fusion
  8.0 1.0 convolution_convert_fusion
  9.0 0.0 copy-start.1
  9.0 173.1 %all-gather.4.cloned.1.call-done = bf16[16384,1024]{1,0:T(8,128)(2,1)} async-done(((bf16[1024,1024]{1,0:T(8,128)(2,1)}), bf16[16384,1024]{1,0:T(8,128)(2,1)}) %all-gather.4.cloned.1.call-update) | async-done | bytes 33554448 | tf_op jit(solution)/shard_map/all_gather | solution.py:30
  182.1 0.0 copy-done
  182.1 18.8 %fusion.2 = f32[16384,64]{0,1:T(8,128)} fusion(bf16[256,64]{1,0:T(8,128)(2,1)S(1)} %convolution_convert_fusion, bf16[16384,1024]{1,0:T(8,128)(2,1)} %all-gather.4.cloned.1.call-done, bf16[256,1024]{1,0:T(8,128)(2,1)S(1)} %copy-done), kind=kOutput, calls=%fused_computation.3 | convolution fusion | flops 9135194112 | bytes 38305792 | tf_op jit(solution)/shard_map/dot_general | solution.py:19
  201.0 0.0 reduce-scatter.2.cloned.1.call-update
  201.0 0.0 all-gather.6.cloned.1.call-start
  201.1 70.5 %reduce-scatter.2.cloned.1.call-done = f32[1024,64]{0,1:T(8,128)} async-done(((f32[16384,64]{0,1:T(8,128)}), f32[1024,64]{0,1:T(8,128)}) %reduce-scatter.2.cloned.1.call-update) | async-done | bytes 262160 | tf_op jit(solution)/shard_map/reduce_scatter | solution.py:31
  271.5 0.0 all-gather.6.cloned.1.call-update
  271.6 0.0 copy-done.1
  271.6 55.3 %all-gather.6.cloned.1.call-done = f32[8192,64]{0,1:T(8,128)} async-done(((f32[1024,64]{0,1:T(8,128)}), f32[8192,64]{0,1:T(8,128)}) %all-gather.6.cloned.1.call-update) | async-done | bytes 2097168 | tf_op jit(solution)/shard_map/all_gather | solution.py:11
  326.9 2.8 copy.7
  329.6 0.5 bitcast_reduce_fusion
  330.2 0.8 broadcast_multiply_fusion
  (1 shorter events, 0.0 us)
Async XLA Ops:
  6.5 175.6 %copy-start = (bf16[256,1024]{1,0:T(8,128)(2,1)S(1)}, bf16[256,1024]{1,0:T(8,128)(2,1)}, u32[]{:S(2)}) copy-start(bf16[256,1024]{1,0:T(8,128)(2,1)} %param.7) | copy-start | bytes 1572868
  6.5 175.6 %all-gather.4.cloned.1.call-start = ((), (), s32[]{:S(2)}) async-start(), calls=%async_computation.1 | async-start | bytes 35651584 | tf_op jit(solution)/shard_map/all_gather | solution.py:30
  7.3 264.3 %reduce-scatter.2.cloned.1.call-start = ((), (), s32[]{:S(2)}) async-start(), calls=%async_computation.2 | async-start | bytes 4456448 | tf_op jit(solution)/shard_map/reduce_scatter | solution.py:31
  9.0 262.5 %copy-start.1 = (f32[64]{0:T(128)S(1)}, f32[64]{0:T(128)}, u32[]{:S(2)}) copy-start(f32[64]{0:T(128)} %param.11) | copy-start | bytes 772
  201.0 125.8 %all-gather.6.cloned.1.call-start = ((), (), s32[]{:S(2)}) async-start(), calls=%async_computation.3 | async-start | bytes 2359296 | tf_op jit(solution)/shard_map/all_gather | solution.py:11
Sparse Core Ops, SparseCore 0:
  9.1 173.0 all-gather.3
  201.1 70.3 reduce-scatter.1
  273.8 52.9 all-gather.5

commit v2 on v0

--- a/solution.py
+++ b/solution.py
@@ -3,8 +3,15 @@
 import jax.numpy as jnp
 from jax import lax
 from jax.sharding import PartitionSpec as P
+from jax.lax import all_to_all, axis_size
 
 BLOCK = 128
+
+
+def cover_series(matrix, group_axis="sl"):
+    return jnp.concatenate(
+        all_to_all(jnp.stack([matrix] * axis_size(group_axis)), group_axis, 0, 0), axis=0
+    )
 
 
 def affinity_sum(rows, land_piece, vec_piece, coeff):
@@ -21,7 +28,7 @@
     rows_scale = jnp.repeat(scale, BLOCK)
     basis = (codes.astype(jnp.float32) * rows_scale[:, None]).astype(jnp.bfloat16)
     vectors = jnp.dot(basis, eigvec, preferred_element_type=jnp.float32).astype(jnp.bfloat16)
-    terms = affinity_sum(lax.all_gather(slab, "sl", axis=0, tiled=True), landmarks, vectors, coeff)
+    terms = affinity_sum(cover_series(slab), landmarks, vectors, coeff)
     partial_sum = lax.psum_scatter(terms, "sl", scatter_dimension=0, tiled=True)
     summed = lax.psum(partial_sum, "lm")
     return summed * factor[None, :]

time: 366 us -> 574 us (1.57)
  waiting for transfers between devices: 330 us -> 521 us
  local copies, waits for them, and re-layouts: 0.08 us -> 12.3 us
  starting transfers between devices: 0.08 us -> 6.18 us
    all_to_all x0 -> x1, waiting for transfers between devices: none -> 365 us  [cover_series(): all_to_all(jnp.stack([matrix] * axis_size(group_axis)), group_axis, 0, 0)]
    all_gather x1 -> x0, waiting for transfers between devices: 173 us -> none  [local(): lax.all_gather(slab, 'sl', axis=0, tiled=True)]
    another operation x0 -> x1, local copies, waits for them, and re-layouts: none -> 12.2 us  [cover_series(): jnp.stack([matrix] * axis_size(group_axis))]
    all_to_all x0 -> x1, starting transfers between devices: none -> 6.09 us  [cover_series(): all_to_all(jnp.stack([matrix] * axis_size(group_axis)), group_axis, 0, 0)]
where the time goes in v2:
time: 574 us
  waiting for transfers between devices  521 us (91%)
  matrix products  19.1 us (3%)
  between operations  13.5 us (2%)
  local copies, waits for them, and re-layouts  12.3 us (2%)
  starting transfers between devices  6.18 us (1%)
    all_to_all x1, waiting for transfers between devices, cover_series(): all_to_all(jnp.stack([matrix] * axis_size(group_axis)), group_axis, 0, 0)  365 us
    psum x1, waiting for transfers between devices, local(): summed = lax.psum(partial_sum, 'lm')  86.2 us
    reduce_scatter x1, waiting for transfers between devices, local(): partial_sum = lax.psum_scatter(terms, 'sl', scatter_dimension=0, tiled=True)  70.2 us
    dot_general x1, matrix products, affinity_sum(): return jnp.dot(affinity, vec_piece, preferred_element_type=jnp.float32)  18.9 us
    another operation x1, local copies, waits for them, and re-layouts, cover_series(): jnp.stack([matrix] * axis_size(group_axis))  12.2 us
  transfers between devices with their start and end apart: 3, of which 3 were waited for; matrix products, arithmetic and copies ran while one was open for 0% of the time, Pallas kernels for 0%

profile of v2, /device:TPU:0, one launch (start us, length us, event | category | flops | bytes accessed | tf_op | source)
XLA Modules:
  0.0 573.8 jit_solution(6835796730593689424)
XLA Ops:
  6.5 0.0 copy-start
  6.5 12.2 %stack.2 = bf16[16,1024,1024]{2,1,0:T(8,128)(2,1)} broadcast(bf16[1024,1024]{1,0:T(8,128)(2,1)} %param.6), dimensions={1,2} | broadcast | bytes 35651584 | tf_op jit(solution)/shard_map/stack | solution.py:13
  18.8 0.0 copy-start.3
  18.8 0.0 copy-start.1
  18.8 0.0 copy-start.2
  18.8 6.1 %all-to-all-start = ((bf16[16,1024,1024]{2,1,0:T(8,128)(2,1)}), bf16[16,1024,1024]{2,1,0:T(8,128)(2,1)}, u32[]{:S(2)}, u32[]{:S(2)}) async-start(bf16[16,1024,1024]{2,1,0:T(8,128)(2,1)} %stack.2), calls=%async_computation | async-start | bytes 67108864 | tf_op jit(solution)/shard_map/all_to_all | solution.py:13
  24.9 0.0 reduce-scatter.2.cloned.1.call-start
  24.9 0.0 copy-done.3
  25.0 0.1 broadcast_bitcast_fusion
  25.0 0.0 copy-done.1
  25.0 0.0 copy-done.2
  25.0 0.2 convolution_convert_fusion
  25.2 364.6 %all-to-all-done = bf16[16,1024,1024]{2,1,0:T(8,128)(2,1)} async-done(((bf16[16,1024,1024]{2,1,0:T(8,128)(2,1)}), bf16[16,1024,1024]{2,1,0:T(8,128)(2,1)}, u32[]{:S(2)}, u32[]{:S(2)}) %all-to-all-start) | async-done | bytes 33554464 | tf_op jit(solution)/shard_map/all_to_all | solution.py:13
  389.9 0.0 copy-done
  389.9 0.0 copy-start.4
  389.9 18.9 %fusion.2 = f32[16384,64]{0,1:T(8,128)} fusion(bf16[256,64]{1,0:T(8,128)(2,1)S(1)} %convolution_convert_fusion, bf16[16384,1024]{1,0:T(8,128)(2,1)} %bitcast, bf16[256,1024]{1,0:T(8,128)(2,1)S(1)} %copy-done), kind=kOutput, calls=%fused_computation.3 | convolution fusion | flops 9135194112 | bytes 38305792 | tf_op jit(solution)/shard_map/dot_general | solution.py:20
  408.7 0.0 reduce-scatter.2.cloned.1.call-update
  408.8 0.0 all-reduce.2.cloned.1.call-start
  408.8 70.2 %reduce-scatter.2.cloned.1.call-done = f32[1024,64]{0,1:T(8,128)} async-done(((f32[16384,64]{0,1:T(8,128)}), f32[1024,64]{0,1:T(8,128)}) %reduce-scatter.2.cloned.1.call-update) | async-done | bytes 262160 | tf_op jit(solution)/shard_map/reduce_scatter | solution.py:32
  479.0 0.0 all-reduce.2.cloned.1.call-update
  479.0 0.0 copy-done.4
  479.1 86.2 %all-reduce.2.cloned.1.call-done = f32[1024,64]{0,1:T(8,128)} async-done(((f32[1024,64]{0,1:T(8,128)}), f32[1024,64]{0,1:T(8,128)}) %all-reduce.2.cloned.1.call-update) | async-done | bytes 262160 | tf_op jit(solution)/shard_map/psum | solution.py:33
  565.2 1.7 broadcast_multiply_fusion
  (2 shorter events, 0.0 us)
Async XLA Ops:
  6.5 383.3 %copy-start = (bf16[256,1024]{1,0:T(8,128)(2,1)S(1)}, bf16[256,1024]{1,0:T(8,128)(2,1)}, u32[]{:S(2)}) copy-start(bf16[256,1024]{1,0:T(8,128)(2,1)} %param.7) | copy-start | bytes 1572868
  18.8 6.2 %copy-start.3 = (s32[2]{0:T(128)S(1)}, s32[2]{0:T(128)}, u32[]{:S(2)}) copy-start(s32[2]{0:T(128)} %param.9) | copy-start | bytes 28
  18.8 6.3 %copy-start.1 = (bf16[256,96]{0,1:T(8,128)(2,1)S(1)}, bf16[256,96]{0,1:T(8,128)(2,1)}, u32[]{:S(2)}) copy-start(bf16[256,96]{0,1:T(8,128)(2,1)} %param.8) | copy-start | bytes 147460
  18.8 6.3 %copy-start.2 = (bf16[96,64]{0,1:T(8,128)(2,1)S(1)}, bf16[96,64]{0,1:T(8,128)(2,1)}, u32[]{:S(2)}) copy-start(bf16[96,64]{0,1:T(8,128)(2,1)} %param.10) | copy-start | bytes 36868
  18.8 371.1 %all-to-all-start = ((bf16[16,1024,1024]{2,1,0:T(8,128)(2,1)}), bf16[16,1024,1024]{2,1,0:T(8,128)(2,1)}, u32[]{:S(2)}, u32[]{:S(2)}) async-start(bf16[16,1024,1024]{2,1,0:T(8,128)(2,1)} %stack.2), calls=%async_computation | async-start | bytes 67108864 | tf_op jit(solution)/shard_map/all_to_all | solution.py:13
  24.9 454.1 %reduce-scatter.2.cloned.1.call-start = ((), (), s32[]{:S(2)}) async-start(), calls=%async_computation.2 | async-start | bytes 4456448 | tf_op jit(solution)/shard_map/reduce_scatter | solution.py:32
  389.9 89.2 %copy-start.4 = (f32[64]{0:T(128)S(1)}, f32[64]{0:T(128)}, u32[]{:S(2)}) copy-start(f32[64]{0:T(128)} %param.11) | copy-start | bytes 772
  408.8 156.5 %all-reduce.2.cloned.1.call-start = ((), (), s32[]{:S(2)}) async-start(), calls=%async_computation.3 | async-start | bytes 524288 | tf_op jit(solution)/shard_map/psum | solution.py:33
Sparse Core Ops, SparseCore 0:
  408.9 70.0 reduce-scatter.1
  481.5 83.7 all-reduce.1
